TPU v7x, 32 devices: a whole 2x2x4 slice. The times are simulated.
32 devices in a mesh: gx: 4 (over z), gy: 4 (over x, core), gz: 2 (over y).
Axes of the slice: x: 2, y: 2, z: 4, core: 2. Of those that a mesh axis runs over, the one named last changes fastest.
Arguments:
- x_a: bfloat16 [32, 8, 64, 256], P(None, 'gx', 'gy', 'gz'), may hold values from -12 to 12
- x_b: bfloat16 [32, 8, 64, 256], P(None, 'gx', 'gy', 'gz'), may hold values from -12 to 12
- w_first: bfloat16 [3, 3, 3, 32, 32], replicated, may hold values from -0.21875 to 0.21875
- w_second: bfloat16 [3, 3, 3, 32, 32], replicated, may hold values from -0.21875 to 0.21875
- gain_first: float32 [32], replicated, may hold values from 0.1 to 1.9
- bias_first: float32 [32], replicated, may hold values from -2 to 2
- gain_second: float32 [32], replicated, may hold values from 0.1 to 1.9
- bias_second: float32 [32], replicated, may hold values from -2 to 2
- grad_out: bfloat16 [32, 8, 64, 256], P(None, 'gx', 'gy', 'gz'), may hold values from -6 to 6
Outputs:
- y_a: bfloat16 [32, 8, 64, 256], P(None, 'gx', 'gy', 'gz')
- dx_b: bfloat16 [32, 8, 64, 256], P(None, 'gx', 'gy', 'gz')
- grad_w_first: float32 [3, 3, 3, 32, 32], replicated
- grad_w_second: float32 [3, 3, 3, 32, 32], replicated
- grad_norm: float32 [4, 32], replicated
All inputs are finite; a program needn't handle non-finite values.
Results may differ from a plain program's by a relative error of at most 0.0063.
Values may be sent and summed in bfloat16 or wider, within the bound.
A program may use at most 128 MiB of HBM per device.

v0:
```python
import math

import jax
import jax.numpy as jnp
from jax import lax
from jax.sharding import PartitionSpec as P

EPSILON = 1e-05


def extended(block, sides, width):
    for axis, dim in sides:
        count = lax.axis_size(axis)
        forward = [(i, i + 1) for i in range(count - 1)]
        backward = [(target, source) for source, target in forward]
        low = lax.ppermute(
            lax.slice_in_dim(block, block.shape[dim] - width, None, axis=dim), axis, forward
        )
        high = lax.ppermute(lax.slice_in_dim(block, 0, width, axis=dim), axis, backward)
        block = jnp.concatenate([low, block, high], axis=dim)
    return block


def spread(values):
    return values[:, None, None, None]


def silu_slope(value):
    sigma = jax.nn.sigmoid(value)
    return sigma * (1.0 + value * (1.0 - sigma))


def convolve(padded, weight):
    in_chan = padded.shape[0]
    out_chan = weight.shape[3]
    span_x = padded.shape[1] - 2
    span_y = padded.shape[2] - 2
    span_z = padded.shape[3] - 2
    total = jnp.zeros((out_chan, span_x * span_y * span_z), jnp.float32)
    for shift_x in range(3):
        for shift_y in range(3):
            pieces = [
                padded[
                    :,
                    shift_x : shift_x + span_x,
                    shift_y : shift_y + span_y,
                    shift_z : shift_z + span_z,
                ]
                for shift_z in range(3)
            ]
            stacked = jnp.concatenate(pieces, axis=0).reshape(3 * in_chan, -1)
            matrix = weight[shift_x, shift_y].transpose(1, 0, 2).reshape(out_chan, 3 * in_chan)
            total = total + jnp.dot(matrix, stacked, preferred_element_type=jnp.float32)
    return total.reshape(out_chan, span_x, span_y, span_z)


def kernel_grad(padded, upstream):
    in_chan = padded.shape[0]
    out_chan = upstream.shape[0]
    span_x, span_y, span_z = (upstream.shape[1], upstream.shape[2], upstream.shape[3])
    flat = upstream.reshape(out_chan, -1)
    rows = []
    for shift_x in range(3):
        for shift_y in range(3):
            pieces = [
                padded[
                    :,
                    shift_x : shift_x + span_x,
                    shift_y : shift_y + span_y,
                    shift_z : shift_z + span_z,
                ]
                for shift_z in range(3)
            ]
            stacked = jnp.concatenate(pieces, axis=0).reshape(3 * in_chan, -1)
            product = lax.dot_general(
                flat, stacked, (((1,), (1,)), ((), ())), preferred_element_type=jnp.float32
            )
            rows.append(product.reshape(out_chan, 3, in_chan).transpose(1, 0, 2))
    return jnp.stack(rows).reshape(3, 3, 3, out_chan, in_chan)


def flipped(weight):
    return jnp.flip(weight, (0, 1, 2)).transpose(0, 1, 2, 4, 3)


def statistics(blocks, voxels):
    local_sums = jnp.stack([jnp.sum(block, axis=(1, 2, 3)) for block in blocks])
    local_squares = jnp.stack([jnp.sum(jnp.square(block), axis=(1, 2, 3)) for block in blocks])
    sums, squares = lax.psum((local_sums, local_squares), ("gx", "gy", "gz"))
    means = sums / voxels
    variance = squares / voxels - means * means
    return (means, lax.rsqrt(variance + EPSILON))


def normalize(block, means, scales, gain, bias):
    normed = (block - spread(means)) * spread(scales)
    return (normed, spread(gain) * normed + spread(bias))


def backward_layer(upstream, preact, normed, scales, gain, voxels):
    slope = upstream * silu_slope(preact)
    sum_d, sum_dx = lax.psum(
        (jnp.sum(slope, axis=(1, 2, 3)), jnp.sum(slope * normed, axis=(1, 2, 3))),
        ("gx", "gy", "gz"),
    )
    delta = spread(gain * scales) * (
        slope - spread(sum_d / voxels) - normed * spread(sum_dx / voxels)
    )
    return (delta.astype(jnp.bfloat16), sum_d, sum_dx)


def body(x_a, x_b, w_first, w_second, gain_first, bias_first, gain_second, bias_second, grad_out):
    rows_x, rows_y, rows_z = (x_a.shape[1], x_a.shape[2], x_a.shape[3])
    voxels = float(
        rows_x * rows_y * rows_z * lax.axis_size("gx") * lax.axis_size("gy") * lax.axis_size("gz")
    )
    factor = 1.0 / math.sqrt(voxels)
    volumes = jnp.stack([x_a, x_b])
    padded = extended(volumes, (("gx", 2), ("gy", 3), ("gz", 4)), 1)
    first = [convolve(padded[member], w_first) for member in range(2)]
    means, scales = statistics(first, voxels)
    hidden = []
    for member in range(2):
        normed, preact = normalize(
            first[member], means[member], scales[member], gain_first, bias_first
        )
        hidden.append((preact * jax.nn.sigmoid(preact)).astype(jnp.bfloat16))
    hidden_all = extended(jnp.stack(hidden), (("gx", 2), ("gy", 3), ("gz", 4)), 1)
    hidden_pads = [hidden_all[0], hidden_all[1]]
    input_pad_b = padded[1]
    scale_one = scales[1]
    second = [convolve(hidden_pads[member], w_second) for member in range(2)]
    means_two, scales_two = statistics(second, voxels)
    normed_a, preact_a = normalize(second[0], means_two[0], scales_two[0], gain_second, bias_second)
    y_a = (preact_a * jax.nn.sigmoid(preact_a)).astype(jnp.bfloat16)
    norm_two, pre_two = normalize(second[1], means_two[1], scales_two[1], gain_second, bias_second)
    delta_two, sum_d2, sum_x2 = backward_layer(
        grad_out.astype(jnp.float32), pre_two, norm_two, scales_two[1], gain_second, voxels
    )
    local_second = kernel_grad(hidden_pads[1], delta_two) * factor
    grad_w_second = lax.psum(local_second, ("gx", "gy", "gz"))
    delta_pad_two = extended(delta_two, (("gx", 1), ("gy", 2), ("gz", 3)), 1)
    upstream_one = convolve(delta_pad_two, flipped(w_second))
    delta_one, sum_d1, sum_x1 = backward_layer(
        upstream_one, preact, normed, scale_one, gain_first, voxels
    )
    local_first = kernel_grad(input_pad_b, delta_one) * factor
    delta_pad_one = extended(delta_one, (("gx", 1), ("gy", 2), ("gz", 3)), 1)
    dx_b = convolve(delta_pad_one, flipped(w_first)).astype(jnp.bfloat16)
    grad_w_first = lax.psum(local_first, ("gx", "gy", "gz"))
    grad_norm = jnp.stack([sum_x1, sum_d1, sum_x2, sum_d2]) * factor
    return (y_a, dx_b, grad_w_first, grad_w_second, grad_norm)


def solution(mesh):
    placed = (
        P(None, "gx", "gy", "gz"),
        P(None, "gx", "gy", "gz"),
        P(),
        P(),
        P(),
        P(),
        P(),
        P(),
        P(None, "gx", "gy", "gz"),
    )
    return jax.shard_map(
        body,
        mesh=mesh,
        in_specs=placed,
        out_specs=(P(None, "gx", "gy", "gz"), P(None, "gx", "gy", "gz"), P(), P(), P()),
        check_vma=False,
    )
```

profile of v0, /device:TPU:0, one launch (start us, length us, event | category | flops | bytes accessed | tf_op | source)
XLA Modules:
  0.0 585.4 jit_solution(11531565275628670312)
XLA Ops:
  8.4 5.0 collective-permute-start
  15.6 3.3 collective-permute-done
  18.9 4.1 collective-permute-done.1
  23.2 3.7 copy.460
  31.5 3.1 collective-permute-done.3
  34.6 6.2 %pad_maximum_fusion = bf16[2,32,4,18,128]{1,2,4,3,0:T(4,128)(2,1)S(1)} fusion(bf16[2,32,4,1,128]{1,2,4,3,0:T(4,128)(2,1)S(1)} %collective-permute-done.3, bf16[2,32,4,16,128]{1,2,4,3,0:T(4,128)(2,1)} %copy.460, bf16[2,32,4,1,128]{1,2,4,3,0:T(4,128)(2,1)S(1)} %collective-permute-done.2), kind=kLoop, calls=%fused_computation | loop fusion | flops 1179648 | bytes 2359296 | tf_op jit(solution)/shard_map/concatenate | solution.py:20
  40.8 2.1 copy-done
  43.0 4.0 collective-permute-start.4
  54.2 6.3 %copy.464 = bf16[2,32,4,18,128]{4,1,3,2,0:T(8,128)(2,1)S(1)} copy(bf16[2,32,4,18,128]{1,2,4,3,0:T(4,128)(2,1)} %copy-done) | data formatting | bytes 2359296 | tf_op jit(solution)/shard_map/concatenate | solution.py:20
  61.5 1.7 copy.463
  66.0 1.7 fusion.176
  67.7 3.2 fusion.175
  82.2 1.6 pad_maximum_fusion.19
  94.8 44.5 %all-reduce.3 = (f32[2,32]{1,0:T(2,128)S(1)}, f32[2,32]{1,0:T(2,128)S(1)}) all-reduce(f32[2,32]{1,0:T(2,128)S(1)} %pad_maximum_fusion.75, f32[2,32]{1,0:T(2,128)S(1)} %pad_maximum_fusion.74), channel_id=1, replica_groups=mesh['gx'=4,'gy'=4,'gz'=2] {'gx','gy','gz'}, use_global_device_ids=true, to_apply=%region_5.0 | all-reduce | flops 128 | bytes 1024 | tf_op jit(solution)/shard_map/psum | solution.py:89
  141.6 2.2 collective-permute-start.6
  145.9 2.7 collective-permute-done.6
  148.5 4.1 collective-permute-done.7
  153.8 5.6 copy.493
  159.4 2.1 fusion.165
  169.8 6.3 %pad_maximum_fusion.1 = bf16[2,32,4,18,128]{1,2,4,3,0:T(4,128)(2,1)S(1)} fusion(bf16[2,32,4,1,128]{1,2,4,3,0:T(4,128)(2,1)} %collective-permute-done.9, bf16[2,32,4,16,128]{1,2,4,3,0:T(4,128)(2,1)} %copy.493, bf16[2,32,4,1,128]{1,2,4,3,0:T(4,128)(2,1)S(1)} %collective-permute-done.8), kind=kLoop, calls=%fused_computation.1 | loop fusion | flops 1179648 | bytes 2359296 | tf_op jit(solution)/shard_map/concatenate | solution.py:20
  176.1 2.1 copy-done.1
  178.3 3.6 collective-permute-start.10
  185.6 2.2 dot_general.394
  195.3 7.1 %copy.497 = bf16[2,32,4,18,128]{4,1,3,2,0:T(8,128)(2,1)} copy(bf16[2,32,4,18,128]{1,2,4,3,0:T(4,128)(2,1)} %copy-done.1) | data formatting | bytes 2359296 | tf_op jit(solution)/shard_map/concatenate | solution.py:20
  204.4 2.6 pad_maximum_fusion.3
  207.2 1.8 fusion.174
  209.0 3.1 fusion.173
  213.3 3.0 fusion.171
  243.7 2.2 dot_general.408
  249.7 2.2 dot_general.404
  257.3 44.2 %all-reduce.2 = (f32[2,32]{1,0:T(2,128)S(1)}, f32[2,32]{1,0:T(2,128)S(1)}) all-reduce(f32[2,32]{1,0:T(2,128)S(1)} %pad_maximum_fusion.77, f32[2,32]{1,0:T(2,128)S(1)} %pad_maximum_fusion.76), channel_id=1, replica_groups=mesh['gx'=4,'gy'=4,'gz'=2] {'gx','gy','gz'}, use_global_device_ids=true, to_apply=%region_11.0 | all-reduce | flops 128 | bytes 1024 | tf_op jit(solution)/shard_map/psum | solution.py:89
  301.7 1.9 fusion.162
  303.6 38.6 %all-reduce.1 = (f32[32]{0:T(128)S(1)}, f32[32]{0:T(128)S(1)}) all-reduce(f32[32]{0:T(128)S(1)} %get-tuple-element.28, f32[32]{0:T(128)S(1)} %get-tuple-element.27), channel_id=1, replica_groups=mesh['gx'=4,'gy'=4,'gz'=2] {'gx','gy','gz'}, use_global_device_ids=true, to_apply=%region_15.0 | all-reduce | flops 64 | bytes 512 | tf_op jit(solution)/shard_map/psum | solution.py:102
  342.1 1.4 multiply_convert_fusion.1
  345.7 3.7 collective-permute-start.12
  349.4 1.4 collective-permute-start.13
  350.9 1.7 fusion.10
  361.8 2.7 collective-permute-done.15
  368.1 5.1 collective-permute-start.16
  376.8 2.2 maximum_maximum_fusion
  387.8 43.2 %all-reduce = (f32[32]{0:T(128)S(1)}, f32[32]{0:T(128)S(1)}) all-reduce(f32[32]{0:T(128)S(1)} %get-tuple-element.26, f32[32]{0:T(128)S(1)} %get-tuple-element.25), channel_id=1, replica_groups=mesh['gx'=4,'gy'=4,'gz'=2] {'gx','gy','gz'}, use_global_device_ids=true, to_apply=%region_19.20 | all-reduce | flops 64 | bytes 512 | tf_op jit(solution)/shard_map/psum | solution.py:102
  432.1 2.1 collective-permute-start.18
  434.2 1.6 collective-permute-start.19
  445.5 3.7 collective-permute-done.21
  452.2 4.5 collective-permute-start.22
  469.4 105.3 %all-reduce.7.cloned.1.call-done = (f32[3,3,3,32,32]{4,3,2,1,0:T(8,128)}, f32[3,3,3,32,32]{4,3,2,1,0:T(8,128)}) async-done(((f32[3,3,3,32,32]{4,3,2,1,0:T(8,128)}, f32[3,3,3,32,32]{4,3,2,1,0:T(8,128)}), (f32[3,3,3,32,32]{4,3,2,1,0:T(8,128)}, f32[3,3,3,32,32]{4,3,2,1,0:T(8,128)})) %all-reduce.7.cloned.1.call-update) | async-done | bytes 221200 | tf_op jit(solution)/shard_map/psum | solution.py:150
  574.7 1.8 copy.917
  576.5 1.8 copy.918
  (639 shorter events, 157.3 us)
Async XLA Ops:
  7.2 15.9 %copy-start.99 = (bf16[32,2,16,128]{3,2,1,0:T(8,128)(2,1)S(1)}, bf16[32,2,16,128]{3,2,1,0:T(8,128)(2,1)}, u32[]{:S(2)}) copy-start(bf16[32,2,16,128]{3,2,1,0:T(8,128)(2,1)} %param.10) | copy-start | bytes 786436
  7.2 15.9 %copy-start.98 = (bf16[32,2,16,128]{3,2,1,0:T(8,128)(2,1)S(1)}, bf16[32,2,16,128]{3,2,1,0:T(8,128)(2,1)}, u32[]{:S(2)}) copy-start(bf16[32,2,16,128]{3,2,1,0:T(8,128)(2,1)} %param.9) | copy-start | bytes 786436
  7.2 567.6 %all-reduce.7.cloned.1.call-start = ((), (), s32[]{:S(2)}) async-start(), calls=%async_computation | async-start | bytes 1769472 | tf_op jit(solution)/shard_map/psum | solution.py:150
  8.4 10.5 %collective-permute-start = (bf16[2,32,1,16,128]{4,3,2,1,0:T(8,128)(2,1)S(1)}, bf16[2,32,1,16,128]{4,3,2,1,0:T(8,128)(2,1)S(1)}, u32[]{:S(2)}, u32[]{:S(2)}) collective-permute-start(bf16[2,32,1,16,128]{4,3,2,1,0:T(8,128)(2,1)S(1)} %get-tuple-element.227), channel_id=1, source_target_pairs={{0,8},{8,16},{16,24},{1,9},{9,17},{17,25},{2,10},{10,18},{18,26},{... | collective-permute-start | bytes 786440 | tf_op jit(solution)/shard_map/ppermute | solution.py:16
  13.4 9.7 %collective-permute-start.1 = (bf16[2,32,1,16,128]{4,3,2,1,0:T(8,128)(2,1)S(1)}, bf16[2,32,1,16,128]{4,3,2,1,0:T(8,128)(2,1)S(1)}, u32[]{:S(2)}, u32[]{:S(2)}) collective-permute-start(bf16[2,32,1,16,128]{4,3,2,1,0:T(8,128)(2,1)S(1)} %get-tuple-element.228), channel_id=1, source_target_pairs={{8,0},{16,8},{24,16},{9,1},{17,9},{25,17},{10,2},{18,10},{26,18},{... | collective-permute-start | bytes 786440 | tf_op jit(solution)/shard_map/ppermute | solution.py:19
  28.2 3.3 collective-permute-start.2
  29.5 5.1 collective-permute-start.3
  31.5 16.8 %copy-start.100 = (bf16[3,3,3,32,32]{4,3,2,1,0:T(8,128)(2,1)S(1)}, bf16[3,3,3,32,32]{4,3,2,1,0:T(8,128)(2,1)}, u32[]{:S(2)}) copy-start(bf16[3,3,3,32,32]{4,3,2,1,0:T(8,128)(2,1)} %param.11) | copy-start | bytes 165892
  43.0 18.5 %collective-permute-start.4 = (bf16[2,32,4,18,1]{1,2,4,3,0:T(4,128)(2,1)S(1)}, bf16[2,32,4,18,1]{1,2,4,3,0:T(4,128)(2,1)}, u32[]{:S(2)}, u32[]{:S(2)}) collective-permute-start(bf16[2,32,4,18,1]{1,2,4,3,0:T(4,128)(2,1)S(1)} %get-tuple-element.43), channel_id=1, source_target_pairs={{0,1},{2,3},{4,5},{6,7},{8,9},{10,11},{12,13},{14,15},{16,17},{18,... | collective-permute-start | bytes 27656 | tf_op jit(solution)/shard_map/ppermute | solution.py:16
  47.0 13.5 %collective-permute-start.5 = (bf16[2,32,4,18,1]{1,2,4,3,0:T(4,128)(2,1)S(1)}, bf16[2,32,4,18,1]{1,2,4,3,0:T(4,128)(2,1)S(1)}, u32[]{:S(2)}, u32[]{:S(2)}) collective-permute-start(bf16[2,32,4,18,1]{1,2,4,3,0:T(4,128)(2,1)S(1)} %get-tuple-element.44), channel_id=1, source_target_pairs={{1,0},{3,2},{5,4},{7,6},{9,8},{11,10},{13,12},{15,14},{17,16},{19,... | collective-permute-start | bytes 27656 | tf_op jit(solution)/shard_map/ppermute | solution.py:19
  82.2 58.9 %copy-start.21 = (f32[4,8,32,128]{3,2,1,0:T(8,128)}, f32[4,8,32,128]{3,2,1,0:T(8,128)S(1)}, u32[]{:S(2)}) copy-start(f32[4,8,32,128]{3,2,1,0:T(8,128)S(1)} %copy.596) | copy-start | bytes 1572868
  92.2 48.9 %copy-start.147 = (f32[32]{0:T(128)S(1)}, f32[32]{0:T(128)}, u32[]{:S(2)}) copy-start(f32[32]{0:T(128)} %param.14) | copy-start | bytes 388
  92.2 48.9 %copy-start.149 = (f32[32]{0:T(128)S(1)}, f32[32]{0:T(128)}, u32[]{:S(2)}) copy-start(f32[32]{0:T(128)} %param.13) | copy-start | bytes 388
  141.6 6.9 %collective-permute-start.6 = (bf16[2,32,1,16,128]{4,3,2,1,0:T(8,128)(2,1)S(1)}, bf16[2,32,1,16,128]{4,3,2,1,0:T(8,128)(2,1)S(1)}, u32[]{:S(2)}, u32[]{:S(2)}) collective-permute-start(bf16[2,32,1,16,128]{4,3,2,1,0:T(8,128)(2,1)S(1)} %get-tuple-element.225), channel_id=1, source_target_pairs={{0,8},{8,16},{16,24},{1,9},{9,17},{17,25},{2,10},{10,18},{18,26},{... | collective-permute-start | bytes 786440 | tf_op jit(solution)/shard_map/ppermute | solution.py:16
  143.8 8.8 %collective-permute-start.7 = (bf16[2,32,1,16,128]{4,3,2,1,0:T(8,128)(2,1)S(1)}, bf16[2,32,1,16,128]{4,3,2,1,0:T(8,128)(2,1)S(1)}, u32[]{:S(2)}, u32[]{:S(2)}) collective-permute-start(bf16[2,32,1,16,128]{4,3,2,1,0:T(8,128)(2,1)S(1)} %get-tuple-element.226), channel_id=1, source_target_pairs={{8,0},{16,8},{24,16},{9,1},{17,9},{25,17},{10,2},{18,10},{26,18},{... | collective-permute-start | bytes 786440 | tf_op jit(solution)/shard_map/ppermute | solution.py:19
  159.4 9.7 %copy-start.126 = (bf16[32,3,32]{2,0,1:T(8,128)(2,1)S(1)}, bf16[32,3,32]{2,0,1:T(8,128)(2,1)}, u32[]{:S(2)}) copy-start(bf16[32,3,32]{2,0,1:T(8,128)(2,1)} %get-tuple-element.260) | copy-start | bytes 18436
  159.4 9.8 %copy-start.125 = (bf16[32,3,32]{2,0,1:T(8,128)(2,1)S(1)}, bf16[32,3,32]{2,0,1:T(8,128)(2,1)}, u32[]{:S(2)}) copy-start(bf16[32,3,32]{2,0,1:T(8,128)(2,1)} %get-tuple-element.261) | copy-start | bytes 18436
  159.4 9.9 %copy-start.124 = (bf16[32,3,32]{2,0,1:T(8,128)(2,1)S(1)}, bf16[32,3,32]{2,0,1:T(8,128)(2,1)}, u32[]{:S(2)}) copy-start(bf16[32,3,32]{2,0,1:T(8,128)(2,1)} %get-tuple-element.262) | copy-start | bytes 18436
  159.4 10.1 %copy-start.123 = (bf16[32,3,32]{2,0,1:T(8,128)(2,1)S(1)}, bf16[32,3,32]{2,0,1:T(8,128)(2,1)}, u32[]{:S(2)}) copy-start(bf16[32,3,32]{2,0,1:T(8,128)(2,1)} %get-tuple-element.263) | copy-start | bytes 18436
  159.4 10.2 %copy-start.122 = (bf16[32,3,32]{2,0,1:T(8,128)(2,1)S(1)}, bf16[32,3,32]{2,0,1:T(8,128)(2,1)}, u32[]{:S(2)}) copy-start(bf16[32,3,32]{2,0,1:T(8,128)(2,1)} %get-tuple-element.264) | copy-start | bytes 18436
  159.4 10.3 %copy-start.121 = (bf16[32,3,32]{2,0,1:T(8,128)(2,1)S(1)}, bf16[32,3,32]{2,0,1:T(8,128)(2,1)}, u32[]{:S(2)}) copy-start(bf16[32,3,32]{2,0,1:T(8,128)(2,1)} %get-tuple-element.265) | copy-start | bytes 18436
  161.5 8.3 %collective-permute-start.8 = (bf16[2,32,4,1,128]{1,2,4,3,0:T(4,128)(2,1)}, bf16[2,32,4,1,128]{1,2,4,3,0:T(4,128)(2,1)S(1)}, u32[]{:S(2)}, u32[]{:S(2)}) collective-permute-start(bf16[2,32,4,1,128]{1,2,4,3,0:T(4,128)(2,1)} %get-tuple-element.45), channel_id=1, source_target_pairs={{0,2},{2,4},{4,6},{1,3},{3,5},{5,7},{8,10},{10,12},{12,14},{9,11},... | collective-permute-start | bytes 196616 | tf_op jit(solution)/shard_map/ppermute | solution.py:16
  162.8 7.0 %collective-permute-start.9 = (bf16[2,32,4,1,128]{1,2,4,3,0:T(4,128)(2,1)}, bf16[2,32,4,1,128]{1,2,4,3,0:T(4,128)(2,1)}, u32[]{:S(2)}, u32[]{:S(2)}) collective-permute-start(bf16[2,32,4,1,128]{1,2,4,3,0:T(4,128)(2,1)} %get-tuple-element.46), channel_id=1, source_target_pairs={{2,0},{4,2},{6,4},{3,1},{5,3},{7,5},{10,8},{12,10},{14,12},{11,9},... | collective-permute-start | bytes 196616 | tf_op jit(solution)/shard_map/ppermute | solution.py:19
  169.8 13.4 %copy-start.146 = (f32[2,32]{1,0:T(2,128)S(1)}, f32[2,32]{1,0:T(2,128)}, u32[]{:S(2)}) copy-start(f32[2,32]{1,0:T(2,128)} %copy-done.145) | copy-start | bytes 772
  169.8 13.4 %copy-start.150 = (f32[32]{0:T(128)S(1)}, f32[32]{0:T(128)}, u32[]{:S(2)}) copy-start(f32[32]{0:T(128)} %param.13) | copy-start | bytes 388
  178.3 25.1 %collective-permute-start.10 = (bf16[2,32,4,18,1]{1,2,4,3,0:T(4,128)(2,1)S(1)}, bf16[2,32,4,18,1]{1,2,4,3,0:T(4,128)(2,1)S(1)}, u32[]{:S(2)}, u32[]{:S(2)}) collective-permute-start(bf16[2,32,4,18,1]{1,2,4,3,0:T(4,128)(2,1)S(1)} %get-tuple-element.41), channel_id=1, source_target_pairs={{0,1},{2,3},{4,5},{6,7},{8,9},{10,11},{12,13},{14,15},{16,17},{18,... | collective-permute-start | bytes 27656 | tf_op jit(solution)/shard_map/ppermute | solution.py:16
  181.9 20.5 %collective-permute-start.11 = (bf16[2,32,4,18,1]{1,2,4,3,0:T(4,128)(2,1)S(1)}, bf16[2,32,4,18,1]{1,2,4,3,0:T(4,128)(2,1)S(1)}, u32[]{:S(2)}, u32[]{:S(2)}) collective-permute-start(bf16[2,32,4,18,1]{1,2,4,3,0:T(4,128)(2,1)S(1)} %get-tuple-element.42), channel_id=1, source_target_pairs={{1,0},{3,2},{5,4},{7,6},{9,8},{11,10},{13,12},{15,14},{17,16},{19,... | collective-permute-start | bytes 27656 | tf_op jit(solution)/shard_map/ppermute | solution.py:19
  256.6 44.9 %copy-start.152 = (f32[32]{0:T(128)S(1)}, f32[32]{0:T(128)}, u32[]{:S(2)}) copy-start(f32[32]{0:T(128)} %param.15) | copy-start | bytes 388
  256.6 45.1 %copy-start.106 = (bf16[32,2,16,128]{3,2,1,0:T(8,128)(2,1)S(1)}, bf16[32,2,16,128]{3,2,1,0:T(8,128)(2,1)}, u32[]{:S(2)}) copy-start(bf16[32,2,16,128]{3,2,1,0:T(8,128)(2,1)} %param.17) | copy-start | bytes 786436
  256.6 45.1 %copy-start.151 = (f32[32]{0:T(128)S(1)}, f32[32]{0:T(128)}, u32[]{:S(2)}) copy-start(f32[32]{0:T(128)} %param.16) | copy-start | bytes 388
  257.2 44.5 %copy-start.43 = (f32[4,8,32,128]{3,2,1,0:T(8,128)S(1)}, f32[4,8,32,128]{3,2,1,0:T(8,128)}, u32[]{:S(2)}) copy-start(f32[4,8,32,128]{3,2,1,0:T(8,128)} %copy.606) | copy-start | bytes 1572868
  344.3 8.3 %copy-start.33 = (bf16[3,32,4096]{2,1,0:T(8,128)(2,1)S(1)}, bf16[3,32,4096]{2,1,0:T(8,128)(2,1)}, u32[]{:S(2)}) copy-start(bf16[3,32,4096]{2,1,0:T(8,128)(2,1)} %dot_general.398) | copy-start | bytes 2359300
  345.5 7.7 %copy-start.36 = (bf16[3,32,4096]{2,1,0:T(8,128)(2,1)S(1)}, bf16[3,32,4096]{2,1,0:T(8,128)(2,1)}, u32[]{:S(2)}) copy-start(bf16[3,32,4096]{2,1,0:T(8,128)(2,1)} %dot_general.400) | copy-start | bytes 2359300
  345.7 11.9 %collective-permute-start.12 = (bf16[32,1,16,128]{3,0,2,1:T(8,128)(2,1)}, bf16[32,1,16,128]{3,0,2,1:T(8,128)(2,1)S(1)}, u32[]{:S(2)}, u32[]{:S(2)}) collective-permute-start(bf16[32,1,16,128]{3,0,2,1:T(8,128)(2,1)} %get-tuple-element.237), channel_id=1, source_target_pairs={{0,8},{8,16},{16,24},{1,9},{9,17},{17,25},{2,10},{10,18},{18,26},{... | collective-permute-start | bytes 393224 | tf_op jit(solution)/shard_map/ppermute | solution.py:16
  349.4 8.2 %collective-permute-start.13 = (bf16[32,1,16,128]{3,0,2,1:T(8,128)(2,1)S(1)}, bf16[32,1,16,128]{3,0,2,1:T(8,128)(2,1)S(1)}, u32[]{:S(2)}, u32[]{:S(2)}) collective-permute-start(bf16[32,1,16,128]{3,0,2,1:T(8,128)(2,1)S(1)} %get-tuple-element.238), channel_id=1, source_target_pairs={{8,0},{16,8},{24,16},{9,1},{17,9},{25,17},{10,2},{18,10},{26,18},{... | collective-permute-start | bytes 393224 | tf_op jit(solution)/shard_map/ppermute | solution.py:19
  357.6 4.2 collective-permute-start.14
  358.9 5.6 collective-permute-start.15
  361.8 11.4 %copy-start.104 = (bf16[32,4,1,128]{3,0,2,1:T(8,128)(2,1)}, bf16[32,4,1,128]{3,0,2,1:T(8,128)(2,1)S(1)}, u32[]{:S(2)}) copy-start(bf16[32,4,1,128]{3,0,2,1:T(8,128)(2,1)S(1)} %collective-permute-done.14) | copy-start | bytes 98308
  364.5 8.7 %copy-start.105 = (bf16[32,4,1,128]{3,0,2,1:T(8,128)(2,1)}, bf16[32,4,1,128]{3,0,2,1:T(8,128)(2,1)S(1)}, u32[]{:S(2)}) copy-start(bf16[32,4,1,128]{3,0,2,1:T(8,128)(2,1)S(1)} %collective-permute-done.15) | copy-start | bytes 98308
  366.8 8.7 %collective-permute-start.17 = (bf16[32,4,18,1]{0,2,3,1:T(8,128)(2,1)S(1)}, bf16[32,4,18,1]{0,2,3,1:T(8,128)(2,1)}, u32[]{:S(2)}, u32[]{:S(2)}) collective-permute-start(bf16[32,4,18,1]{0,2,3,1:T(8,128)(2,1)S(1)} %copy.531), channel_id=1, source_target_pairs={{1,0},{3,2},{5,4},{7,6},{9,8},{11,10},{13,12},{15,14},{17,16},{19,... | collective-permute-start | bytes 13832 | tf_op jit(solution)/shard_map/ppermute | solution.py:19
  368.1 6.8 %collective-permute-start.16 = (bf16[32,4,18,1]{0,2,3,1:T(8,128)(2,1)}, bf16[32,4,18,1]{0,2,3,1:T(8,128)(2,1)S(1)}, u32[]{:S(2)}, u32[]{:S(2)}) collective-permute-start(bf16[32,4,18,1]{0,2,3,1:T(8,128)(2,1)} %copy.529), channel_id=1, source_target_pairs={{0,1},{2,3},{4,5},{6,7},{8,9},{10,11},{12,13},{14,15},{16,17},{18,... | collective-permute-start | bytes 13832 | tf_op jit(solution)/shard_map/ppermute | solution.py:16
  387.8 43.5 %copy-start.22 = (f32[4,8,32,128]{3,2,1,0:T(8,128)S(1)}, f32[4,8,32,128]{3,2,1,0:T(8,128)}, u32[]{:S(2)}) copy-start(f32[4,8,32,128]{3,2,1,0:T(8,128)} %copy-done.21) | copy-start | bytes 1572868
  432.1 10.2 %collective-permute-start.18 = (bf16[32,1,16,128]{3,0,2,1:T(8,128)(2,1)S(1)}, bf16[32,1,16,128]{3,0,2,1:T(8,128)(2,1)S(1)}, u32[]{:S(2)}, u32[]{:S(2)}) collective-permute-start(bf16[32,1,16,128]{3,0,2,1:T(8,128)(2,1)S(1)} %get-tuple-element.232), channel_id=1, source_target_pairs={{0,8},{8,16},{16,24},{1,9},{9,17},{17,25},{2,10},{10,18},{18,26},{... | collective-permute-start | bytes 393224 | tf_op jit(solution)/shard_map/ppermute | solution.py:16
  434.2 8.1 %collective-permute-start.19 = (bf16[32,1,16,128]{3,0,2,1:T(8,128)(2,1)S(1)}, bf16[32,1,16,128]{3,0,2,1:T(8,128)(2,1)S(1)}, u32[]{:S(2)}, u32[]{:S(2)}) collective-permute-start(bf16[32,1,16,128]{3,0,2,1:T(8,128)(2,1)S(1)} %get-tuple-element.233), channel_id=1, source_target_pairs={{8,0},{16,8},{24,16},{9,1},{17,9},{25,17},{10,2},{18,10},{26,18},{... | collective-permute-start | bytes 393224 | tf_op jit(solution)/shard_map/ppermute | solution.py:19
  442.3 3.2 collective-permute-start.20
  443.6 5.6 collective-permute-start.21
  450.9 7.9 %collective-permute-start.23 = (bf16[32,4,18,1]{0,2,3,1:T(8,128)(2,1)S(1)}, bf16[32,4,18,1]{0,2,3,1:T(8,128)(2,1)S(1)}, u32[]{:S(2)}, u32[]{:S(2)}) collective-permute-start(bf16[32,4,18,1]{0,2,3,1:T(8,128)(2,1)S(1)} %copy.546), channel_id=1, source_target_pairs={{1,0},{3,2},{5,4},{7,6},{9,8},{11,10},{13,12},{15,14},{17,16},{19,... | collective-permute-start | bytes 13832 | tf_op jit(solution)/shard_map/ppermute | solution.py:19
  452.2 6.1 %collective-permute-start.22 = (bf16[32,4,18,1]{0,2,3,1:T(8,128)(2,1)S(1)}, bf16[32,4,18,1]{0,2,3,1:T(8,128)(2,1)S(1)}, u32[]{:S(2)}, u32[]{:S(2)}) collective-permute-start(bf16[32,4,18,1]{0,2,3,1:T(8,128)(2,1)S(1)} %copy.544), channel_id=1, source_target_pairs={{0,1},{2,3},{4,5},{6,7},{8,9},{10,11},{12,13},{14,15},{16,17},{18,... | collective-permute-start | bytes 13832 | tf_op jit(solution)/shard_map/ppermute | solution.py:16
  (130 other events, 218.3 us)
Sparse Core Ops, SparseCore 0:
  442.4 132.2 all-reduce.6
where the time goes:
time: 592 us; the launch traced here: 585 us
  blocking collectives  170 us (29%)
  local copies, waits for them, and re-layouts  139 us (23%)
  waiting for transfers between devices  131 us (22%)
  starting transfers between devices  51.5 us (9%)
  other arithmetic  40.1 us (7%)
  matrix products  36.3 us (6%)
  between operations  17.5 us (3%)
    psum x1, waiting for transfers between devices, body(): grad_w_first = lax.psum(local_first, ('gx', 'gy', 'gz'))  105 us
    psum x2, blocking collectives, statistics(): sums, squares = lax.psum((local_sums, local_squares), ('gx', 'gy', 'gz'))  88.7 us
    psum x2, blocking collectives, backward_layer(): lax.psum((jnp.sum(slope, axis=(1, 2, 3)), jnp.sum(slope * normed, axis=(1...  81.7 us
    ppermute x12, starting transfers between devices, extended(): lax.ppermute(lax.slice_in_dim(block, block.shape[dim] - width, None, axis...  35.5 us
    dot_general x18, local copies, waits for them, and re-layouts, kernel_grad(): lax.dot_general(flat, stacked, (((1,), (1,)), ((), ())), preferred_elemen...  25 us
    dot_general x54, matrix products, convolve(): total = total + jnp.dot(matrix, stacked, preferred_element_type=jnp.float32)  24.8 us
    unnamed x315, local copies, waits for them, and re-layouts  23.4 us
    concatenate x4, local copies, waits for them, and re-layouts, extended(): block = jnp.concatenate([low, block, high], axis=dim)  22.8 us
  transfers between devices with their start and end apart: 25, of which 10 were waited for; matrix products, arithmetic and copies ran while one was open for 12% of the time, Pallas kernels for 0%

commit v1 on v0

v1 whole, which is shorter than its diff:
```python
import functools
import math

import jax
import jax.numpy as jnp
from jax import lax
from jax.experimental import pallas as pl
from jax.experimental.pallas import tpu as pltpu
from jax.sharding import PartitionSpec as P

EPSILON = 1e-05
AXES = ("gx", "gy", "gz")
MESH = pl.DeviceIdType.MESH


def slope_of(z):
    s = jax.nn.sigmoid(z)
    return s * (1.0 + z * (1.0 - s))


def kernel(
    sizes, voxels,
    xa, xb, go, w1, w2, w1t, w2t, g1, b1, g2, b2,
    ya, dxb, gw1, gw2, gnorm,
    pads, edge_out, edge_in, shift_a, shift_xb, shift_hb, shift_d,
    c1a, c1b, c2a, c2b, d2, d1, stat, wbuf, wacc,
    halo_send, halo_recv, sum_send, sum_recv, w_send, w_recv,
):
    nx, ny, chan, nz = xa.shape
    half = ny // 2
    wide = ny + 2
    me = [lax.axis_index(a) for a in AXES]
    factor = 1.0 / math.sqrt(voxels)
    lane = lax.broadcasted_iota(jnp.int32, (chan, nz), 1)
    zero = jnp.zeros((chan, nz), jnp.float32)

    def peers(k):
        n = sizes[k]
        return [(d, lax.rem(me[k] + d, n), lax.rem(me[k] + n - d, n)) for d in range(1, n)]

    barrier = pltpu.get_barrier_semaphore()
    count = 0
    for k in range(3):
        for _, to, _ in peers(k):
            pl.semaphore_signal(barrier, inc=1, device_id={AXES[k]: to}, device_id_type=MESH)
            count += 1
    pl.semaphore_wait(barrier, count)

    def halo_refs(v, k):
        p = pads.at[v]
        if k == 0:
            rows = pl.ds(1, ny)
            return (p.at[nx, rows], p.at[0, rows]), (p.at[1, rows], p.at[nx + 1, rows])
        if k == 1:
            return (p.at[:, ny], p.at[:, 0]), (p.at[:, 1], p.at[:, ny + 1])
        return (edge_out.at[v, 0], edge_in.at[v, 0]), (edge_out.at[v, 1], edge_in.at[v, 1])

    def halo_copy(v, k, side):
        src, dst = halo_refs(v, k)[side]
        return pltpu.make_async_remote_copy(
            src_ref=src, dst_ref=dst, send_sem=halo_send.at[v, k, side],
            recv_sem=halo_recv.at[v, k, side], device_id={AXES[k]: me[k] + 1 - 2 * side},
            device_id_type=MESH)

    def halo_start(v, k):
        n = sizes[k]
        (_, up_dst), (_, down_dst) = halo_refs(v, k)

        @pl.when(me[k] < n - 1)
        def _():
            halo_copy(v, k, 0).start()

        @pl.when(me[k] > 0)
        def _():
            halo_copy(v, k, 1).start()

        @pl.when(me[k] == 0)
        def _():
            up_dst[...] = jnp.zeros(up_dst.shape, up_dst.dtype)

        @pl.when(me[k] == n - 1)
        def _():
            down_dst[...] = jnp.zeros(down_dst.shape, down_dst.dtype)

    def halo_wait(v, k):
        n = sizes[k]

        @pl.when(me[k] < n - 1)
        def _():
            halo_copy(v, k, 0).wait_send()
            halo_copy(v, k, 1).wait_recv()

        @pl.when(me[k] > 0)
        def _():
            halo_copy(v, k, 1).wait_send()
            halo_copy(v, k, 0).wait_recv()

    def pack(v):
        def step(x, carry):
            low, high = carry
            for y in range(wide):
                tile = pads[v, x, y].astype(jnp.float32)
                here = lane == x * wide + y
                high = jnp.where(here, tile[:, nz - 1:nz], high)
                low = jnp.where(here, tile[:, 0:1], low)
            return low, high
        low, high = lax.fori_loop(0, nx + 2, step, (zero, zero))
        edge_out[v, 0] = high.astype(jnp.bfloat16)
        edge_out[v, 1] = low.astype(jnp.bfloat16)

    def unpack(v, shifted):
        low = edge_in[v, 0].astype(jnp.float32)
        high = pltpu.roll(edge_in[v, 1].astype(jnp.float32), nz - 1, 1)

        def step(x, carry):
            low, high = carry
            for y in range(wide):
                row = x * wide + y
                own = pads[v, x, y]
                tile = own.astype(jnp.float32)
                shifted[row, 0:chan] = jnp.where(
                    lane == 0, low, pltpu.roll(tile, 1, 1)).astype(jnp.bfloat16)
                shifted[row, chan:2 * chan] = own
                shifted[row, 2 * chan:] = jnp.where(
                    lane == nz - 1, high, pltpu.roll(tile, nz - 1, 1)).astype(jnp.bfloat16)
                low = pltpu.roll(low, nz - 1, 1)
                high = pltpu.roll(high, nz - 1, 1)
            return low, high
        lax.fori_loop(0, nx + 2, step, (low, high))

    def halo_rest(todo):
        for v, _ in todo:
            halo_wait(v, 0)
        for v, _ in todo:
            halo_start(v, 1)
        for v, _ in todo:
            halo_wait(v, 1)
        for v, _ in todo:
            pack(v)
            halo_start(v, 2)
        for v, _ in todo:
            halo_wait(v, 2)
        for v, shifted in todo:
            unpack(v, shifted)

    def stacked(shifted, x, y):
        parts = []
        for tx in range(3):
            for ty in range(3):
                row = (x + tx) * wide + y + ty
                parts.append(jnp.concatenate([shifted[row], shifted[row + 1]], axis=1))
        return jnp.concatenate(parts, axis=0)

    def place(i):
        return i // half, (i % half) * 2

    def row_loop(body, init):
        def step(i, carry):
            x, y = i // (ny // 4), (i % (ny // 4)) * 4
            for u in range(4):
                carry = body(x, y + u, carry)
            return carry
        return lax.fori_loop(0, nx * (ny // 4), step, init)

    def total(value):
        return jnp.sum(value, axis=1, keepdims=True)

    def tile_of(values):
        tile = zero
        for at, value in enumerate(values):
            tile = jnp.where(lane == at, value, tile)
        return tile

    def all_sum(slots, k, send, recv):
        def copy(at, to, frm):
            return pltpu.make_async_remote_copy(
                src_ref=slots.at[at], dst_ref=slots.at[at], send_sem=send.at[to],
                recv_sem=recv.at[at], device_id={AXES[k]: to}, device_id_type=MESH)

        def start():
            for _, to, frm in peers(k):
                copy(me[k], to, frm).start()

        def finish():
            for _, to, frm in peers(k):
                copy(me[k], to, frm).wait_send()
                copy(frm, to, frm).wait_recv()
        return start, finish

    def reduce_stats(j, tile):
        for k in range(3):
            slots = stat.at[j, k]
            slots[me[k]] = tile
            start, finish = all_sum(slots, k, sum_send.at[j, k], sum_recv.at[j, k])
            start()
            finish()
            tile = slots[0]
            for r in range(1, sizes[k]):
                tile = tile + slots[r]
        return tile

    def weight_start(j, k, value):
        slots = wbuf.at[j, k]
        slots[me[k]] = value.astype(jnp.bfloat16)
        all_sum(slots, k, w_send.at[j, k], w_recv.at[j, k])[0]()

    def weight_finish(j, k):
        slots = wbuf.at[j, k]
        all_sum(slots, k, w_send.at[j, k], w_recv.at[j, k])[1]()
        value = slots[0].astype(jnp.float32)
        for r in range(1, sizes[k]):
            value = value + slots[r].astype(jnp.float32)
        return value

    def conv_stats(shift_one, shift_two, w, out_one, out_two):
        def step(i, carry):
            x, y = place(i)
            new = []
            for n, (shifted, out) in enumerate(((shift_one, out_one), (shift_two, out_two))):
                o = jnp.dot(w[...], stacked(shifted, x, y), preferred_element_type=jnp.float32)
                left, right = o[:, :nz], o[:, nz:]
                out[x, y] = left
                out[x, y + 1] = right
                new.append(carry[2 * n] + left + right)
                new.append(carry[2 * n + 1] + left * left + right * right)
            return tuple(new)
        return lax.fori_loop(0, nx * half, step, (zero,) * 4)

    def norm(tile, at):
        mean = tile[:, at:at + 1] / voxels
        var = tile[:, at + 1:at + 2] / voxels - mean * mean
        return jnp.broadcast_to(mean, zero.shape), jnp.broadcast_to(
            lax.rsqrt(var + EPSILON), zero.shape)

    def wgrad(v, shifted):
        wacc[...] = jnp.zeros(wacc.shape, jnp.float32)

        def step(i, carry):
            x, y = place(i)
            delta = jnp.concatenate([pads[v, x + 1, y + 1], pads[v, x + 1, y + 2]], axis=1)
            wacc[...] += lax.dot_general(
                delta, stacked(shifted, x, y), (((1,), (1,)), ((), ())),
                preferred_element_type=jnp.float32)
            return carry
        lax.fori_loop(0, nx * half, step, 0)

    def fill(x, y, carry):
        pads[0, x + 1, y + 1] = xa[x, y]
        pads[1, x + 1, y + 1] = xb[x, y]
        return carry
    row_loop(fill, 0)
    halo_start(0, 0)
    halo_start(1, 0)
    halo_rest(((0, shift_a), (1, shift_xb)))
    sums = conv_stats(shift_a, shift_xb, w1, c1a, c1b)
    tile = reduce_stats(0, tile_of([total(s) for s in sums]))
    mean_a, scale_a = norm(tile, 0)
    mean_one, scale_one = norm(tile, 2)
    gain_one = jnp.broadcast_to(g1[...], zero.shape)
    bias_one = jnp.broadcast_to(b1[...], zero.shape)
    gain_two = jnp.broadcast_to(g2[...], zero.shape)
    bias_two = jnp.broadcast_to(b2[...], zero.shape)

    def silu(z):
        return (z * jax.nn.sigmoid(z)).astype(jnp.bfloat16)

    def hidden(x, y, carry):
        za = gain_one * ((c1a[x, y] - mean_a) * scale_a) + bias_one
        pads[2, x + 1, y + 1] = silu(za)
        nb = (c1b[x, y] - mean_one) * scale_one
        c1b[x, y] = nb
        pads[3, x + 1, y + 1] = silu(gain_one * nb + bias_one)
        return carry
    row_loop(hidden, 0)
    halo_start(2, 0)
    halo_start(3, 0)
    halo_rest(((2, shift_a), (3, shift_hb)))
    sums = conv_stats(shift_a, shift_hb, w2, c2a, c2b)
    tile = reduce_stats(1, tile_of([total(s) for s in sums]))
    mean_a2, scale_a2 = norm(tile, 0)
    mean_two, scale_two = norm(tile, 2)

    def slope_two(x, y, carry):
        sd, sx = carry
        nb = (c2b[x, y] - mean_two) * scale_two
        c2b[x, y] = nb
        d = go[x, y].astype(jnp.float32) * slope_of(gain_two * nb + bias_two)
        d2[x, y] = d
        return sd + d, sx + d * nb
    sd, sx = row_loop(slope_two, (zero, zero))
    tile2 = reduce_stats(2, tile_of([total(sx), total(sd)]))
    sx2 = jnp.broadcast_to(tile2[:, 0:1] / voxels, zero.shape)
    sd2 = jnp.broadcast_to(tile2[:, 1:2] / voxels, zero.shape)

    def delta_two(x, y, carry):
        pads[4, x + 1, y + 1] = ((gain_two * scale_two) * (
            d2[x, y] - sd2 - c2b[x, y] * sx2)).astype(jnp.bfloat16)
        return carry
    row_loop(delta_two, 0)
    halo_start(4, 0)
    wgrad(4, shift_hb)

    def finish_a(x, y, carry):
        ya[x, y] = silu(gain_two * ((c2a[x, y] - mean_a2) * scale_a2) + bias_two)
        return carry
    row_loop(finish_a, 0)
    halo_rest(((4, shift_d),))
    weight_start(0, 0, wacc[...])

    def back(i, carry):
        x, y = place(i)
        sd, sx = carry
        o = jnp.dot(w2t[...], stacked(shift_d, x, y), preferred_element_type=jnp.float32)
        for u in range(2):
            nb = c1b[x, y + u]
            d = o[:, u * nz:(u + 1) * nz] * slope_of(gain_one * nb + bias_one)
            d1[x, y + u] = d
            sd, sx = sd + d, sx + d * nb
        return sd, sx
    sd, sx = lax.fori_loop(0, nx * half, back, (zero, zero))
    weight_start(0, 1, weight_finish(0, 0))
    tile1 = reduce_stats(3, tile_of([total(sx), total(sd)]))
    sx1 = jnp.broadcast_to(tile1[:, 0:1] / voxels, zero.shape)
    sd1 = jnp.broadcast_to(tile1[:, 1:2] / voxels, zero.shape)
    gnorm[...] = tile_of(
        [tile1[:, 0:1], tile1[:, 1:2], tile2[:, 0:1], tile2[:, 1:2]]) * factor

    def delta_one(x, y, carry):
        pads[5, x + 1, y + 1] = ((gain_one * scale_one) * (
            d1[x, y] - sd1 - c1b[x, y] * sx1)).astype(jnp.bfloat16)
        return carry
    row_loop(delta_one, 0)
    halo_start(5, 0)
    wgrad(5, shift_xb)
    weight_start(0, 2, weight_finish(0, 1))
    halo_rest(((5, shift_d),))
    weight_start(1, 0, wacc[...])

    def last(i, carry):
        x, y = place(i)
        o = jnp.dot(w1t[...], stacked(shift_d, x, y), preferred_element_type=jnp.float32)
        for u in range(2):
            dxb[x, y + u] = o[:, u * nz:(u + 1) * nz].astype(jnp.bfloat16)
        return carry
    lax.fori_loop(0, nx * half, last, 0)
    weight_start(1, 1, weight_finish(1, 0))
    gw2[...] = weight_finish(0, 2) * factor
    weight_start(1, 2, weight_finish(1, 1))
    gw1[...] = weight_finish(1, 2) * factor


def body(sizes, x_a, x_b, w_first, w_second, gain_first, bias_first, gain_second, bias_second,
         grad_out):
    chan, nx, ny, nz = x_a.shape
    voxels = float(nx * ny * nz * math.prod(sizes))
    taps = 27 * chan

    def rows(block):
        return block.transpose(1, 2, 0, 3)

    def matrix(w):
        return w.reshape(27, chan, chan).transpose(1, 0, 2).reshape(chan, taps)

    def flipped(w):
        return jnp.flip(w, (0, 1, 2)).transpose(0, 1, 2, 4, 3)

    def column(v):
        return v.reshape(chan, 1)

    most = max(sizes)
    bf16, f32 = jnp.bfloat16, jnp.float32
    span = (nx + 2) * (ny + 2)
    grid = (nx, ny, chan, nz)
    vmem = pl.BlockSpec(memory_space=pltpu.VMEM)
    dma = pltpu.SemaphoreType.DMA
    y_a, dx_b, gw1, gw2, gnorm = pl.pallas_call(
        functools.partial(kernel, sizes, voxels),
        out_shape=(
            jax.ShapeDtypeStruct(grid, bf16),
            jax.ShapeDtypeStruct(grid, bf16),
            jax.ShapeDtypeStruct((chan, taps), f32),
            jax.ShapeDtypeStruct((chan, taps), f32),
            jax.ShapeDtypeStruct((chan, nz), f32),
        ),
        in_specs=[vmem] * 11,
        out_specs=[vmem] * 5,
        scratch_shapes=[
            pltpu.VMEM((6, nx + 2, ny + 2, chan, nz), bf16),
            pltpu.VMEM((6, 2, chan, nz), bf16),
            pltpu.VMEM((6, 2, chan, nz), bf16),
        ] + [pltpu.VMEM((span, 3 * chan, nz), bf16)] * 4
        + [pltpu.VMEM(grid, f32)] * 6
        + [
            pltpu.VMEM((4, 3, most, chan, nz), f32),
            pltpu.VMEM((2, 3, most, chan, taps), bf16),
            pltpu.VMEM((chan, taps), f32),
            dma((6, 3, 2)), dma((6, 3, 2)),
            dma((4, 3, most)), dma((4, 3, most)),
            dma((2, 3, most)), dma((2, 3, most)),
        ],
        compiler_params=pltpu.CompilerParams(
            collective_id=0, has_side_effects=True, vmem_limit_bytes=50 * 1024 * 1024),
    )(
        rows(x_a), rows(x_b), rows(grad_out),
        matrix(w_first), matrix(w_second), matrix(flipped(w_first)), matrix(flipped(w_second)),
        column(gain_first), column(bias_first), column(gain_second), column(bias_second),
    )

    def tensor(g):
        return g.reshape(chan, 27, chan).transpose(1, 0, 2).reshape(3, 3, 3, chan, chan)

    return (
        y_a.transpose(2, 0, 1, 3), dx_b.transpose(2, 0, 1, 3),
        tensor(gw1), tensor(gw2), gnorm[:, :4].T,
    )


def solution(mesh):
    sizes = tuple(mesh.shape[a] for a in AXES)
    split = P(None, *AXES)
    return jax.shard_map(
        functools.partial(body, sizes),
        mesh=mesh,
        in_specs=(split, split, P(), P(), P(), P(), P(), P(), split),
        out_specs=(split, split, P(), P(), P()),
        check_vma=False,
    )
```

time: 592 us -> 162 us (0.27)
  blocking collectives: 170 us -> 0 us
  Pallas kernels: 0 us -> 147 us
  waiting for transfers between devices: 131 us -> 0 us
  local copies, waits for them, and re-layouts: 139 us -> 13.4 us
  starting transfers between devices: 51.5 us -> 0 us
  other arithmetic: 40.1 us -> 0 us
  matrix products: 36.3 us -> 0 us
  between operations: 17.5 us -> 0.76 us
    psum x4 -> x0, blocking collectives: 170 us -> none  [the longest x2 88.7 us: statistics(): sums, squares = lax.psum((local_sums, local_squares), ('gx', 'gy', 'gz'))]
    pallas_call x0 -> x1, Pallas kernels: none -> 147 us  [body(): pl.pallas_call(functools.partial(kernel, sizes, voxels), out_shape=(jax.S...]
    psum x1 -> x0, waiting for transfers between devices: 105 us -> none  [body(): grad_w_first = lax.psum(local_first, ('gx', 'gy', 'gz'))]
    ppermute x24 -> x0, starting transfers between devices: 51.5 us -> none  [the longest x12 35.5 us: extended(): lax.ppermute(lax.slice_in_dim(block, block.shape[dim] - width, None, axis...]
    concatenate x58 -> x0, local copies, waits for them, and re-layouts: 42 us -> none  [the longest x4 22.8 us: extended(): block = jnp.concatenate([low, block, high], axis=dim)]
    dot_general x72 -> x0, matrix products: 36.3 us -> none  [the longest x54 24.8 us: convolve(): total = total + jnp.dot(matrix, stacked, preferred_element_type=jnp.float32)]
    concatenate x56 -> x0, other arithmetic: 30.3 us -> none  [the longest x12 21.6 us: extended(): block = jnp.concatenate([low, block, high], axis=dim)]
    slice x29 -> x0, local copies, waits for them, and re-layouts: 27.6 us -> none  [the longest x15 18.5 us: convolve(): padded[:, shift_x:shift_x + span_x, shift_y:shift_y + span_y, shift_z:shi...]
  transfers between devices with their start and end apart: 25 -> 0, of which waited for: 10 -> 0; matrix products, arithmetic and copies ran while one was open for 12% -> 0% of each run, Pallas kernels for 0% -> 0%
where the time goes in v1:
time: 162 us; the launch traced here: 161 us
  Pallas kernels  147 us (91%)
  local copies, waits for them, and re-layouts  13.4 us (8%)
    pallas_call x1, Pallas kernels, body(): pl.pallas_call(functools.partial(kernel, sizes, voxels), out_shape=(jax.S...  147 us
    unnamed x22, local copies, waits for them, and re-layouts  7.51 us

profile of v1, /device:TPU:0, one launch (start us, length us, event | category | flops | bytes accessed | tf_op | source)
XLA Modules:
  0.0 161.3 jit_solution(10619681431279327198)
XLA Ops:
  0.6 0.0 copy-start.5
  0.6 0.6 copy-done.5
  1.3 0.0 copy-start.6
  1.3 0.1 copy.53.g1
  1.4 0.6 copy-done.6
  1.9 0.0 copy-start.7
  1.9 0.1 copy.54.b1
  2.0 0.6 copy-done.7
  2.6 0.0 copy-start.8
  2.6 0.1 copy.55.g2
  2.7 0.6 copy-done.8
  3.3 0.1 copy.56.b2
  3.3 0.9 rev.7
  4.3 0.4 copy.51
  4.7 0.0 copy-start
  4.7 0.2 reshape.63.w1t
  5.0 0.7 copy-done
  5.7 0.4 copy.52
  6.1 0.0 copy-start.2
  6.1 0.2 reshape.65.w2t
  6.4 0.7 copy-done.2
  7.1 0.1 copy.69
  7.2 0.1 copy.67
  7.3 0.0 copy-start.1
  7.3 0.2 reshape.61.w2
  7.6 0.7 copy-done.1
  8.2 0.0 copy-start.4
  8.2 0.1 copy.68
  8.3 0.0 copy-start.3
  8.3 0.2 reshape.59.w1
  8.6 0.6 copy-done.4
  9.2 0.1 copy-done.3
  9.3 0.2 copy_bitcast_fusion.2
  9.5 147.1 %shard_map.128 = (bf16[2,16,32,128]{3,2,1,0:T(8,128)(2,1)S(1)}, bf16[2,16,32,128]{3,2,1,0:T(8,128)(2,1)S(1)}, f32[32,864]{1,0:T(8,128)S(1)}, f32[32,864]{1,0:T(8,128)S(1)}, f32[32,128]{1,0:T(8,128)S(1)}) custom-call(bf16[2,16,32,128]{3,2,1,0:T(8,128)(2,1)S(1)} %bitcast.35, bf16[2,16,32,128]{3,2,1,0:T(8,128)(2,1)S(1)} %get-tuple-element.31.xb, ...), custom_call_target="tpu_custom_call" | custom-call | tf_op jit(solution)/shard_map/pallas_call | solution.py:376
  156.6 0.8 copy.59
  157.4 0.8 copy.60
  158.2 0.7 copy.61
  158.9 0.2 reshape.70
  159.1 1.0 copy.57
  160.1 0.2 reshape.72
  160.3 1.0 copy.58
  (2 shorter events, 0.0 us)
Async XLA Ops:
  0.6 0.7 copy-start.5
  1.3 0.7 copy-start.6
  1.9 0.7 copy-start.7
  2.6 0.7 copy-start.8
  4.7 0.9 copy-start
  6.1 1.0 copy-start.2
  7.3 0.9 copy-start.1
  8.2 0.9 copy-start.4
  8.3 1.0 copy-start.3

commit v2 on v1

--- a/solution.py
+++ b/solution.py
@@ -22,7 +22,7 @@
     sizes, voxels,
     xa, xb, go, w1, w2, w1t, w2t, g1, b1, g2, b2,
     ya, dxb, gw1, gw2, gnorm,
-    pads, edge_out, edge_in, shift_a, shift_xb, shift_hb, shift_d,
+    pads, edge_out, edge_in, edge_x, bases, shift_a, shift_xb, shift_hb, shift_d,
     c1a, c1b, c2a, c2b, d2, d1, stat, wbuf, wacc,
     halo_send, halo_recv, sum_send, sum_recv, w_send, w_recv,
 ):
@@ -34,15 +34,23 @@
     lane = lax.broadcasted_iota(jnp.int32, (chan, nz), 1)
     zero = jnp.zeros((chan, nz), jnp.float32)
 
+    counts = (sizes[0], sizes[1] * sizes[2])
+    rank = (me[0], me[1] * sizes[2] + me[2])
+
     def peers(k):
-        n = sizes[k]
-        return [(d, lax.rem(me[k] + d, n), lax.rem(me[k] + n - d, n)) for d in range(1, n)]
+        n = counts[k]
+        return [(lax.rem(rank[k] + d, n), lax.rem(rank[k] + n - d, n)) for d in range(1, n)]
+
+    def where(k, at):
+        if k == 0:
+            return {AXES[0]: at}
+        return {AXES[1]: at // sizes[2], AXES[2]: at % sizes[2]}
 
     barrier = pltpu.get_barrier_semaphore()
     count = 0
-    for k in range(3):
-        for _, to, _ in peers(k):
-            pl.semaphore_signal(barrier, inc=1, device_id={AXES[k]: to}, device_id_type=MESH)
+    for k in range(2):
+        for to, _ in peers(k):
+            pl.semaphore_signal(barrier, inc=1, device_id=where(k, to), device_id_type=MESH)
             count += 1
     pl.semaphore_wait(barrier, count)
 
@@ -52,95 +60,114 @@
             rows = pl.ds(1, ny)
             return (p.at[nx, rows], p.at[0, rows]), (p.at[1, rows], p.at[nx + 1, rows])
         if k == 1:
-            return (p.at[:, ny], p.at[:, 0]), (p.at[:, 1], p.at[:, ny + 1])
+            rows = pl.ds(1, nx)
+            return (p.at[rows, ny], p.at[rows, 0]), (p.at[rows, 1], p.at[rows, ny + 1])
+        if k == 3 or k == 4:
+            y = 0 if k == 3 else ny + 1
+            return (p.at[nx, y], p.at[0, y]), (p.at[1, y], p.at[nx + 1, y])
+        if k == 5:
+            return (edge_in.at[v], edge_x.at[v, 0]), (edge_in.at[v], edge_x.at[v, 1])
         return (edge_out.at[v, 0], edge_in.at[v, 0]), (edge_out.at[v, 1], edge_in.at[v, 1])
 
     def halo_copy(v, k, side):
         src, dst = halo_refs(v, k)[side]
         return pltpu.make_async_remote_copy(
             src_ref=src, dst_ref=dst, send_sem=halo_send.at[v, k, side],
-            recv_sem=halo_recv.at[v, k, side], device_id={AXES[k]: me[k] + 1 - 2 * side},
+            recv_sem=halo_recv.at[v, k, side], device_id={AXES[along[k]]: me[along[k]] + 1 - 2 * side},
             device_id_type=MESH)
 
+    along = (0, 1, 2, 0, 0, 0)
+
     def halo_start(v, k):
-        n = sizes[k]
+        here, n = me[along[k]], sizes[along[k]]
         (_, up_dst), (_, down_dst) = halo_refs(v, k)
 
-        @pl.when(me[k] < n - 1)
+        @pl.when(here < n - 1)
         def _():
             halo_copy(v, k, 0).start()
 
-        @pl.when(me[k] > 0)
+        @pl.when(here > 0)
         def _():
             halo_copy(v, k, 1).start()
 
-        @pl.when(me[k] == 0)
+        @pl.when(here == 0)
         def _():
             up_dst[...] = jnp.zeros(up_dst.shape, up_dst.dtype)
 
-        @pl.when(me[k] == n - 1)
+        @pl.when(here == n - 1)
         def _():
             down_dst[...] = jnp.zeros(down_dst.shape, down_dst.dtype)
 
     def halo_wait(v, k):
-        n = sizes[k]
-
-        @pl.when(me[k] < n - 1)
+        here, n = me[along[k]], sizes[along[k]]
+
+        @pl.when(here < n - 1)
         def _():
             halo_copy(v, k, 0).wait_send()
             halo_copy(v, k, 1).wait_recv()
 
-        @pl.when(me[k] > 0)
+        @pl.when(here > 0)
         def _():
             halo_copy(v, k, 1).wait_send()
             halo_copy(v, k, 0).wait_recv()
 
     def pack(v):
-        def step(x, carry):
+        def step(i, carry):
             low, high = carry
+            x = i + 1
             for y in range(wide):
                 tile = pads[v, x, y].astype(jnp.float32)
                 here = lane == x * wide + y
                 high = jnp.where(here, tile[:, nz - 1:nz], high)
                 low = jnp.where(here, tile[:, 0:1], low)
             return low, high
-        low, high = lax.fori_loop(0, nx + 2, step, (zero, zero))
+        low, high = lax.fori_loop(0, nx, step, (zero, zero))
         edge_out[v, 0] = high.astype(jnp.bfloat16)
         edge_out[v, 1] = low.astype(jnp.bfloat16)
 
+    def turned(tile, by):
+        by = by % nz
+        return pltpu.roll(tile, by, 1) if by else tile
+
     def unpack(v, shifted):
-        low = edge_in[v, 0].astype(jnp.float32)
-        high = pltpu.roll(edge_in[v, 1].astype(jnp.float32), nz - 1, 1)
+        for x in range(nx + 2):
+            for side in range(2):
+                if x == 0:
+                    tile, at = edge_x[v, 0, side], nx * wide
+                elif x == nx + 1:
+                    tile, at = edge_x[v, 1, side], wide
+                else:
+                    tile, at = edge_in[v, side], x * wide
+                bases[x, side] = turned(tile.astype(jnp.float32), -at - side)
 
         def step(x, carry):
-            low, high = carry
             for y in range(wide):
                 row = x * wide + y
                 own = pads[v, x, y]
                 tile = own.astype(jnp.float32)
+                low = turned(bases[x, 0], -y)
+                high = turned(bases[x, 1], -y)
                 shifted[row, 0:chan] = jnp.where(
-                    lane == 0, low, pltpu.roll(tile, 1, 1)).astype(jnp.bfloat16)
+                    lane == 0, low, turned(tile, 1)).astype(jnp.bfloat16)
                 shifted[row, chan:2 * chan] = own
                 shifted[row, 2 * chan:] = jnp.where(
-                    lane == nz - 1, high, pltpu.roll(tile, nz - 1, 1)).astype(jnp.bfloat16)
-                low = pltpu.roll(low, nz - 1, 1)
-                high = pltpu.roll(high, nz - 1, 1)
-            return low, high
-        lax.fori_loop(0, nx + 2, step, (low, high))
+                    lane == nz - 1, high, turned(tile, -1)).astype(jnp.bfloat16)
+            return carry
+        lax.fori_loop(0, nx + 2, step, 0)
 
     def halo_rest(todo):
         for v, _ in todo:
-            halo_wait(v, 0)
-        for v, _ in todo:
-            halo_start(v, 1)
-        for v, _ in todo:
             halo_wait(v, 1)
-        for v, _ in todo:
+            halo_start(v, 3)
+            halo_start(v, 4)
             pack(v)
             halo_start(v, 2)
         for v, _ in todo:
             halo_wait(v, 2)
+            halo_start(v, 5)
         for v, shifted in todo:
+            for k in (0, 3, 4, 5):
+                halo_wait(v, k)
             unpack(v, shifted)
 
     def stacked(shifted, x, y):
@@ -175,40 +202,40 @@
         def copy(at, to, frm):
             return pltpu.make_async_remote_copy(
                 src_ref=slots.at[at], dst_ref=slots.at[at], send_sem=send.at[to],
-                recv_sem=recv.at[at], device_id={AXES[k]: to}, device_id_type=MESH)
+                recv_sem=recv.at[at], device_id=where(k, to), device_id_type=MESH)
 
         def start():
-            for _, to, frm in peers(k):
-                copy(me[k], to, frm).start()
+            for to, frm in peers(k):
+                copy(rank[k], to, frm).start()
 
         def finish():
-            for _, to, frm in peers(k):
-                copy(me[k], to, frm).wait_send()
+            for to, frm in peers(k):
+                copy(rank[k], to, frm).wait_send()
                 copy(frm, to, frm).wait_recv()
         return start, finish
 
     def reduce_stats(j, tile):
-        for k in range(3):
+        for k in range(2):
             slots = stat.at[j, k]
-            slots[me[k]] = tile
+            slots[rank[k]] = tile
             start, finish = all_sum(slots, k, sum_send.at[j, k], sum_recv.at[j, k])
             start()
             finish()
             tile = slots[0]
-            for r in range(1, sizes[k]):
+            for r in range(1, counts[k]):
                 tile = tile + slots[r]
         return tile
 
     def weight_start(j, k, value):
         slots = wbuf.at[j, k]
-        slots[me[k]] = value.astype(jnp.bfloat16)
+        slots[rank[k]] = value.astype(jnp.bfloat16)
         all_sum(slots, k, w_send.at[j, k], w_recv.at[j, k])[0]()
 
     def weight_finish(j, k):
         slots = wbuf.at[j, k]
         all_sum(slots, k, w_send.at[j, k], w_recv.at[j, k])[1]()
         value = slots[0].astype(jnp.float32)
-        for r in range(1, sizes[k]):
+        for r in range(1, counts[k]):
             value = value + slots[r].astype(jnp.float32)
         return value
 
@@ -250,7 +277,9 @@
         return carry
     row_loop(fill, 0)
     halo_start(0, 0)
+    halo_start(0, 1)
     halo_start(1, 0)
+    halo_start(1, 1)
     halo_rest(((0, shift_a), (1, shift_xb)))
     sums = conv_stats(shift_a, shift_xb, w1, c1a, c1b)
     tile = reduce_stats(0, tile_of([total(s) for s in sums]))
@@ -273,7 +302,9 @@
         return carry
     row_loop(hidden, 0)
     halo_start(2, 0)
+    halo_start(2, 1)
     halo_start(3, 0)
+    halo_start(3, 1)
     halo_rest(((2, shift_a), (3, shift_hb)))
     sums = conv_stats(shift_a, shift_hb, w2, c2a, c2b)
     tile = reduce_stats(1, tile_of([total(s) for s in sums]))
@@ -298,6 +329,7 @@
         return carry
     row_loop(delta_two, 0)
     halo_start(4, 0)
+    halo_start(4, 1)
     wgrad(4, shift_hb)
 
     def finish_a(x, y, carry):
@@ -331,8 +363,8 @@
         return carry
     row_loop(delta_one, 0)
     halo_start(5, 0)
+    halo_start(5, 1)
     wgrad(5, shift_xb)
-    weight_start(0, 2, weight_finish(0, 1))
     halo_rest(((5, shift_d),))
     weight_start(1, 0, wacc[...])
 
@@ -344,9 +376,8 @@
         return carry
     lax.fori_loop(0, nx * half, last, 0)
     weight_start(1, 1, weight_finish(1, 0))
-    gw2[...] = weight_finish(0, 2) * factor
-    weight_start(1, 2, weight_finish(1, 1))
-    gw1[...] = weight_finish(1, 2) * factor
+    gw2[...] = weight_finish(0, 1) * factor
+    gw1[...] = weight_finish(1, 1) * factor
 
 
 def body(sizes, x_a, x_b, w_first, w_second, gain_first, bias_first, gain_second, bias_second,
@@ -367,7 +398,7 @@
     def column(v):
         return v.reshape(chan, 1)
 
-    most = max(sizes)
+    most = max(sizes[0], sizes[1] * sizes[2])
     bf16, f32 = jnp.bfloat16, jnp.float32
     span = (nx + 2) * (ny + 2)
     grid = (nx, ny, chan, nz)
@@ -388,15 +419,17 @@
             pltpu.VMEM((6, nx + 2, ny + 2, chan, nz), bf16),
             pltpu.VMEM((6, 2, chan, nz), bf16),
             pltpu.VMEM((6, 2, chan, nz), bf16),
+            pltpu.VMEM((6, 2, 2, chan, nz), bf16),
+            pltpu.VMEM((nx + 2, 2, chan, nz), f32),
         ] + [pltpu.VMEM((span, 3 * chan, nz), bf16)] * 4
         + [pltpu.VMEM(grid, f32)] * 6
         + [
-            pltpu.VMEM((4, 3, most, chan, nz), f32),
-            pltpu.VMEM((2, 3, most, chan, taps), bf16),
+            pltpu.VMEM((4, 2, most, chan, nz), f32),
+            pltpu.VMEM((2, 2, most, chan, taps), bf16),
             pltpu.VMEM((chan, taps), f32),
-            dma((6, 3, 2)), dma((6, 3, 2)),
-            dma((4, 3, most)), dma((4, 3, most)),
-            dma((2, 3, most)), dma((2, 3, most)),
+            dma((6, 6, 2)), dma((6, 6, 2)),
+            dma((4, 2, most)), dma((4, 2, most)),
+            dma((2, 2, most)), dma((2, 2, most)),
         ],
         compiler_params=pltpu.CompilerParams(
             collective_id=0, has_side_effects=True, vmem_limit_bytes=50 * 1024 * 1024),

time: 162 us -> 121 us (0.75)
  Pallas kernels: 147 us -> 106 us
    pallas_call x1, Pallas kernels: 147 us -> 106 us  [body(): pl.pallas_call(functools.partial(kernel, sizes, voxels), out_shape=(jax.S...]
where the time goes in v2:
time: 121 us; the launch traced here: 120 us
  Pallas kernels  106 us (88%)
  local copies, waits for them, and re-layouts  13.4 us (11%)
    pallas_call x1, Pallas kernels, body(): pl.pallas_call(functools.partial(kernel, sizes, voxels), out_shape=(jax.S...  106 us
    unnamed x22, local copies, waits for them, and re-layouts  7.51 us

profile of v2, /device:TPU:0, one launch (start us, length us, event | category | flops | bytes accessed | tf_op | source)
XLA Modules:
  0.0 120.2 jit_solution(17815939511130789728)
XLA Ops:
  0.6 0.0 copy-start.5
  0.6 0.6 copy-done.5
  1.3 0.0 copy-start.6
  1.3 0.1 copy.53.g1
  1.4 0.6 copy-done.6
  1.9 0.0 copy-start.7
  1.9 0.1 copy.54.b1
  2.0 0.6 copy-done.7
  2.6 0.0 copy-start.8
  2.6 0.1 copy.55.g2
  2.7 0.6 copy-done.8
  3.3 0.1 copy.56.b2
  3.3 0.9 rev.7
  4.3 0.4 copy.51
  4.7 0.0 copy-start
  4.7 0.2 reshape.63.w1t
  5.0 0.7 copy-done
  5.7 0.4 copy.52
  6.1 0.0 copy-start.2
  6.1 0.2 reshape.65.w2t
  6.4 0.7 copy-done.2
  7.1 0.1 copy.69
  7.2 0.1 copy.67
  7.3 0.0 copy-start.1
  7.3 0.2 reshape.61.w2
  7.6 0.7 copy-done.1
  8.2 0.0 copy-start.4
  8.2 0.1 copy.68
  8.3 0.0 copy-start.3
  8.3 0.2 reshape.59.w1
  8.6 0.6 copy-done.4
  9.2 0.1 copy-done.3
  9.3 0.2 copy_bitcast_fusion.2
  9.5 106.0 %shard_map.128 = (bf16[2,16,32,128]{3,2,1,0:T(8,128)(2,1)S(1)}, bf16[2,16,32,128]{3,2,1,0:T(8,128)(2,1)S(1)}, f32[32,864]{1,0:T(8,128)S(1)}, f32[32,864]{1,0:T(8,128)S(1)}, f32[32,128]{1,0:T(8,128)S(1)}) custom-call(bf16[2,16,32,128]{3,2,1,0:T(8,128)(2,1)S(1)} %bitcast.35, bf16[2,16,32,128]{3,2,1,0:T(8,128)(2,1)S(1)} %get-tuple-element.31.xb, ...), custom_call_target="tpu_custom_call" | custom-call | tf_op jit(solution)/shard_map/pallas_call | solution.py:407
  115.5 0.8 copy.59
  116.3 0.8 copy.60
  117.1 0.7 copy.61
  117.8 0.2 reshape.70
  118.0 1.0 copy.57
  119.0 0.2 reshape.72
  119.2 1.0 copy.58
  (2 shorter events, 0.0 us)
Async XLA Ops:
  0.6 0.7 copy-start.5
  1.3 0.7 copy-start.6
  1.9 0.7 copy-start.7
  2.6 0.7 copy-start.8
  4.7 0.9 copy-start
  6.1 1.0 copy-start.2
  7.3 0.9 copy-start.1
  8.2 0.9 copy-start.4
  8.3 1.0 copy-start.3
